TPU v7x, 32 devices: a whole 2x2x4 slice. The times are simulated.
32 devices in a mesh: grp: 2 (over y), seg: 16 (over z, x, core).
Axes of the slice: x: 2, y: 2, z: 4, core: 2. Of those that a mesh axis runs over, the one named last changes fastest.
Arguments:
- strain: bfloat16 [524288], P(('grp', 'seg')), parts along dimension 0, may hold values from -6 to 6
- templates: bfloat16 [128, 512], P('seg'), may hold values from -6 to 6
Outputs:
- profile: float32 [32, 128], P(('grp', 'seg')), parts along dimension 0
- overall: float32 [256], P('grp'), parts along dimension 0
There are 2 independent parts, one for each index of `grp`. A program takes and returns all parts, laid end to end along the dimension named above; an argument that names none is the same for every part. Nothing has to cross between parts.
All inputs are finite; a program needn't handle non-finite values.
Results may differ from a plain program's by a relative error of at most 0.0003.
Values may be sent and summed in bfloat16 or wider, within the bound.
A program may use at most 256 MiB of HBM per device.

v0:
```python
import jax
import jax.numpy as jnp
from jax import lax
from jax.sharding import PartitionSpec as P

EPSILON = 1e-05


def passed_along(block, axis, distance):
    devices = range(lax.axis_size(axis))
    route = [(i - distance, i) for i in devices if i - distance in devices]
    return lax.ppermute(block, axis, route)


def hankel(extended, width):
    count = (extended.shape[0] - width) // width
    lower = extended[: count * width].reshape(count, width)
    upper = extended[width:].reshape(count, width)
    paired = jnp.concatenate([lower, upper], axis=1)
    tiled = jnp.tile(paired, (1, width + 1))[:, : width * (2 * width + 1)]
    windows = tiled.reshape(count, width, 2 * width + 1)[:, :, :width].reshape(count * width, width)
    return (paired, windows)


def window_stats(paired, width):
    rows = jnp.arange(2 * width)[:, None]
    cols = jnp.arange(width)[None, :]
    ones_band = ((rows >= cols) & (rows < cols + width)).astype(jnp.float32)
    floats = paired.astype(jnp.float32)
    totals = jnp.dot(floats, ones_band, precision=lax.Precision.HIGHEST).reshape(-1)
    squared = jnp.dot(floats * floats, ones_band, precision=lax.Precision.HIGHEST).reshape(-1)
    win_mean = totals / width
    variance = squared / width - win_mean * win_mean
    return (win_mean, jnp.sqrt(jnp.maximum(variance, 0.0) + EPSILON))


def template_minima(windows, win_mean, win_dev, usable, templates):
    width = templates.shape[1]
    floats = templates.astype(jnp.float32)
    t_mean = jnp.mean(floats, axis=1)
    t_dev = jnp.sqrt(jnp.mean((floats - t_mean[:, None]) ** 2, axis=1) + EPSILON)
    products = lax.dot_general(
        windows, templates, (((1,), (1,)), ((), ())), preferred_element_type=jnp.float32
    )
    rho = (products - width * win_mean[:, None] * t_mean[None, :]) / (
        width * win_dev[:, None] * t_dev[None, :]
    )
    distance = jnp.sqrt(jnp.maximum(2.0 - 2.0 * rho, 0.0))
    distance = jnp.where(usable[:, None], distance, jnp.inf)
    return jnp.min(distance, axis=0)


def per_device(strain, templates):
    width = templates.shape[1]
    seg_len = strain.shape[0]
    following = passed_along(strain[:width], "seg", -1)
    extended = jnp.concatenate([strain, following])
    paired, windows = hankel(extended, width)
    win_mean, win_dev = window_stats(paired, width)
    number = lax.axis_index("seg")
    places = number * seg_len + jnp.arange(seg_len, dtype=jnp.int32)
    usable = places <= seg_len * lax.axis_size("seg") - width
    gathered = lax.all_gather(templates, "seg", axis=0, tiled=True)
    minima = template_minima(windows, win_mean, win_dev, usable, gathered)
    profile = minima[None, :]
    collected = lax.all_gather(profile, "seg", axis=0, tiled=True)
    overall = jnp.min(collected, axis=0)
    return (profile, overall)


def solution(mesh):
    in_specs = (P(("grp", "seg")), P("seg", None))
    out_specs = (P(("grp", "seg"), None), P("grp"))
    return jax.shard_map(
        per_device, mesh=mesh, in_specs=in_specs, out_specs=out_specs, check_vma=False
    )
```

profile of v0, /device:TPU:0, one launch (start us, length us, event | category | flops | bytes accessed | tf_op | source)
XLA Modules:
  0.0 228.7 jit_solution(16680242244528655759)
XLA Ops:
  0.6 0.7 slice.22
  1.3 1.3 collective-permute-start
  2.6 0.8 reshape.71
  3.4 24.3 %all_gather.6 = bf16[128,512]{1,0:T(8,128)(2,1)S(1)} all-gather(bf16[8,512]{1,0:T(8,128)(2,1)} %param.3), channel_id=1, replica_groups=mesh['grp'=2,'seg'=16] {'seg'}, dimensions={0}, use_global_device_ids=true | all-gather | bytes 139264 | tf_op jit(solution)/shard_map/all_gather | solution.py:63
  27.7 0.1 convert_reduce_fusion
  27.9 0.2 fusion.24
  28.1 0.0 collective-permute-done
  28.1 0.8 pad_maximum_fusion
  28.9 0.5 fusion.12
  29.4 0.8 fusion.18
  30.3 11.3 %tile.4 = bf16[32,513,1024]{2,1,0:T(8,128)(2,1)} broadcast(bf16[32,1024]{1,0:T(8,128)(2,1)S(1)} %constant_dynamic-update-slice_fusion), dimensions={0,2} | broadcast | bytes 33685504 | tf_op jit(solution)/shard_map/tile | solution.py:20
  41.5 23.4 %copy.4 = bf16[4,8,513,1024]{3,1,2,0:T(8,128)(2,1)} copy(bf16[4,8,513,1024]{3,2,1,0:T(8,128)(2,1)} %bitcast.14) | data formatting | bytes 67239936
  64.9 22.9 %slice.27 = bf16[32,524800]{1,0:T(8,128)(2,1)} slice(bf16[32,525312]{1,0:T(8,128)(2,1)} %bitcast.15), slice={[0:32], [0:524800]} | slice | bytes 67174400 | tf_op jit(solution)/shard_map/slice | solution.py:20
  87.8 108.4 %reshape.72 = bf16[32,512,1025]{2,1,0:T(8,128)(2,1)} reshape(bf16[32,524800]{1,0:T(8,128)(2,1)} %slice.27) | data formatting | bytes 67174400 | tf_op jit(solution)/shard_map/reshape | solution.py:21
  196.2 0.0 slice-start
  196.3 5.7 %slice-done = bf16[32,512,512]{2,1,0:T(8,128)(2,1)S(1)} async-done(((bf16[32,512,1025]{2,1,0:T(8,128)(2,1)}), bf16[32,512,512]{2,1,0:T(8,128)(2,1)S(1)}, s32[]{:S(2)}) %slice-start) | async-done | bytes 16777240 | tf_op jit(solution)/shard_map/slice | solution.py:21
  202.0 8.7 %fusion.7 = f32[128]{0:T(128)S(1)} fusion(f32[128]{0:T(128)S(1)} %add_sqrt_fusion, f32[16384]{0:T(1024)S(1)} %sqrt_multiply_fusion, f32[128]{0:T(128)S(1)} %broadcast_multiply_fusion, f32[16384]{0:T(1024)S(1)} %bitcast.18, bf16[16384,512]{1,0:T(8,128)(2,1)S(1)} %bitcast.16, bf16[128,512]{1,0:T(8,128)(2,1)S(1)} %all_gather.6, ...), kind=kOutput, calls=%fused_computation.10 | convolution fusion | flops 2166358016 | bytes 17057280 | tf_op jit(solution)/shard_map/dot_general | solution.py:42
  210.7 0.0 copy-start
  210.7 17.4 %all-gather.1 = f32[16,1,128]{2,1,0:T(1,128)S(1)} all-gather(f32[1,1,128]{2,1,0:T(1,128)S(1)} %bitcast.20), channel_id=2, replica_groups=mesh['grp'=2,'seg'=16] {'seg'}, dimensions={0}, use_global_device_ids=true | all-gather | bytes 8704 | tf_op jit(solution)/shard_map/all_gather | solution.py:66
  228.2 0.5 reduce_min.19
  228.7 0.0 copy-done
  (10 shorter events, 0.1 us)
Async XLA Ops:
  1.3 26.8 %collective-permute-start = (bf16[512]{0:T(512)(128)(2,1)S(1)}, bf16[512]{0:T(512)(128)(2,1)S(1)}, u32[]{:S(2)}, u32[]{:S(2)}) collective-permute-start(bf16[512]{0:T(512)(128)(2,1)S(1)} %slice.22), channel_id=1, source_target_pairs={{1,0},{2,1},{3,2},{4,3},{5,4},{6,5},{7,6},{8,7},{9,8},{10,9},{11,1... | collective-permute-start | bytes 3080 | tf_op jit(solution)/shard_map/ppermute | solution.py:12
  196.2 5.8 %slice-start = ((bf16[32,512,1025]{2,1,0:T(8,128)(2,1)}), bf16[32,512,512]{2,1,0:T(8,128)(2,1)S(1)}, s32[]{:S(2)}) async-start(bf16[32,512,1025]{2,1,0:T(8,128)(2,1)} %reshape.72), calls=%async_computation | async-start | bytes 33554432 | tf_op jit(solution)/shard_map/slice | solution.py:21
  210.7 18.0 %copy-start = (f32[128]{0:T(128)}, f32[128]{0:T(128)S(1)}, u32[]{:S(2)}) copy-start(f32[128]{0:T(128)S(1)} %fusion.7) | copy-start | bytes 1540
where the time goes:
time: 229 us
  local copies, waits for them, and re-layouts  173 us (76%)
  blocking collectives  41.8 us (18%)
  matrix products  9.95 us (4%)
    reshape x1, local copies, waits for them, and re-layouts, hankel(): tiled.reshape(count, width, 2 * width + 1)[:, :, :width]  108 us
    all_gather x1, blocking collectives, per_device(): gathered = lax.all_gather(templates, 'seg', axis=0, tiled=True)  24.3 us
    unnamed x6, local copies, waits for them, and re-layouts  23.4 us
    slice x1, local copies, waits for them, and re-layouts, hankel(): tiled = jnp.tile(paired, (1, width + 1))[:, :width * (2 * width + 1)]  22.9 us
    all_gather x1, blocking collectives, per_device(): collected = lax.all_gather(profile, 'seg', axis=0, tiled=True)  17.4 us
    another operation x1, local copies, waits for them, and re-layouts, hankel(): tiled = jnp.tile(paired, (1, width + 1))[:, :width * (2 * width + 1)]  11.3 us
    dot_general x1, matrix products, template_minima(): lax.dot_general(windows, templates, (((1,), (1,)), ((), ())), preferred_e...  8.69 us
    slice x2, local copies, waits for them, and re-layouts, hankel(): tiled.reshape(count, width, 2 * width + 1)[:, :, :width]  5.73 us
  transfers between devices with their start and end apart: 1, of which 0 were waited for; matrix products, arithmetic and copies ran while one was open for 0% of the time, Pallas kernels for 0%

commit v1 on v0

--- a/solution.py
+++ b/solution.py
@@ -63,7 +63,10 @@
     gathered = lax.all_gather(templates, "seg", axis=0, tiled=True)
     minima = template_minima(windows, win_mean, win_dev, usable, gathered)
     profile = minima[None, :]
-    collected = lax.all_gather(profile, "seg", axis=0, tiled=True)
+    count_2 = lax.axis_size("seg")
+    blocks = jnp.stack([profile for _ in range(count_2)])
+    blocks = lax.all_to_all(blocks, "seg", split_axis=0, concat_axis=0)
+    collected = jnp.concatenate(blocks, axis=0)
     overall = jnp.min(collected, axis=0)
     return (profile, overall)
 

time: 229 us -> 221 us (0.965)
  blocking collectives: 41.8 us -> 33.3 us
    all_gather x1 -> x0, blocking collectives: 17.4 us -> none  [per_device(): collected = lax.all_gather(profile, 'seg', axis=0, tiled=True)]
    all_to_all x0 -> x1, blocking collectives: none -> 9.01 us  [per_device(): blocks = lax.all_to_all(blocks, 'seg', split_axis=0, concat_axis=0)]
  transfers between devices with their start and end apart: 1 -> 1, of which waited for: 0 -> 0; matrix products, arithmetic and copies ran while one was open for 0% -> 1% of each run, Pallas kernels for 0% -> 0%
where the time goes in v1:
time: 221 us; the launch traced here: 220 us
  local copies, waits for them, and re-layouts  173 us (78%)
  blocking collectives  33.3 us (15%)
  matrix products  9.95 us (5%)
    reshape x1, local copies, waits for them, and re-layouts, hankel(): tiled.reshape(count, width, 2 * width + 1)[:, :, :width]  108 us
    all_gather x1, blocking collectives, per_device(): gathered = lax.all_gather(templates, 'seg', axis=0, tiled=True)  24.3 us
    unnamed x6, local copies, waits for them, and re-layouts  23.4 us
    slice x1, local copies, waits for them, and re-layouts, hankel(): tiled = jnp.tile(paired, (1, width + 1))[:, :width * (2 * width + 1)]  22.9 us
    another operation x1, local copies, waits for them, and re-layouts, hankel(): tiled = jnp.tile(paired, (1, width + 1))[:, :width * (2 * width + 1)]  11.3 us
    all_to_all x1, blocking collectives, per_device(): blocks = lax.all_to_all(blocks, 'seg', split_axis=0, concat_axis=0)  9.01 us
    dot_general x1, matrix products, template_minima(): lax.dot_general(windows, templates, (((1,), (1,)), ((), ())), preferred_e...  8.69 us
    slice x2, local copies, waits for them, and re-layouts, hankel(): tiled.reshape(count, width, 2 * width + 1)[:, :, :width]  5.73 us
  transfers between devices with their start and end apart: 1, of which 0 were waited for; matrix products, arithmetic and copies ran while one was open for 1% of the time, Pallas kernels for 0%

profile of v1, /device:TPU:0, one launch (start us, length us, event | category | flops | bytes accessed | tf_op | source)
XLA Modules:
  0.0 220.3 jit_solution(5956024881237796135)
XLA Ops:
  0.6 0.7 slice.22
  1.3 1.3 collective-permute-start
  2.6 0.8 reshape.74
  3.4 24.3 %all_gather.3 = bf16[128,512]{1,0:T(8,128)(2,1)S(1)} all-gather(bf16[8,512]{1,0:T(8,128)(2,1)} %param.3), channel_id=1, replica_groups=mesh['grp'=2,'seg'=16] {'seg'}, dimensions={0}, use_global_device_ids=true | all-gather | bytes 139264 | tf_op jit(solution)/shard_map/all_gather | solution.py:63
  27.7 0.1 convert_reduce_fusion
  27.9 0.2 fusion.24
  28.1 0.0 collective-permute-done
  28.1 0.8 pad_maximum_fusion
  28.9 0.5 fusion.12
  29.4 0.8 fusion.18
  30.3 11.3 %tile.4 = bf16[32,513,1024]{2,1,0:T(8,128)(2,1)} broadcast(bf16[32,1024]{1,0:T(8,128)(2,1)S(1)} %constant_dynamic-update-slice_fusion), dimensions={0,2} | broadcast | bytes 33685504 | tf_op jit(solution)/shard_map/tile | solution.py:20
  41.5 23.4 %copy.5 = bf16[4,8,513,1024]{3,1,2,0:T(8,128)(2,1)} copy(bf16[4,8,513,1024]{3,2,1,0:T(8,128)(2,1)} %bitcast.14) | data formatting | bytes 67239936
  64.9 22.9 %slice.27 = bf16[32,524800]{1,0:T(8,128)(2,1)} slice(bf16[32,525312]{1,0:T(8,128)(2,1)} %bitcast.15), slice={[0:32], [0:524800]} | slice | bytes 67174400 | tf_op jit(solution)/shard_map/slice | solution.py:20
  87.8 108.4 %reshape.75 = bf16[32,512,1025]{2,1,0:T(8,128)(2,1)} reshape(bf16[32,524800]{1,0:T(8,128)(2,1)} %slice.27) | data formatting | bytes 67174400 | tf_op jit(solution)/shard_map/reshape | solution.py:21
  196.2 0.0 slice-start
  196.3 5.7 %slice-done = bf16[32,512,512]{2,1,0:T(8,128)(2,1)S(1)} async-done(((bf16[32,512,1025]{2,1,0:T(8,128)(2,1)}), bf16[32,512,512]{2,1,0:T(8,128)(2,1)S(1)}, s32[]{:S(2)}) %slice-start) | async-done | bytes 16777240 | tf_op jit(solution)/shard_map/slice | solution.py:21
  202.0 8.7 %fusion.7 = f32[128]{0:T(128)S(1)} fusion(f32[128]{0:T(128)S(1)} %add_sqrt_fusion, f32[16384]{0:T(1024)S(1)} %sqrt_multiply_fusion, f32[128]{0:T(128)S(1)} %broadcast_multiply_fusion, f32[16384]{0:T(1024)S(1)} %bitcast.18, bf16[16384,512]{1,0:T(8,128)(2,1)S(1)} %bitcast.16, bf16[128,512]{1,0:T(8,128)(2,1)S(1)} %all_gather.3, ...), kind=kOutput, calls=%fused_computation.10 | convolution fusion | flops 2166358016 | bytes 17057280 | tf_op jit(solution)/shard_map/dot_general | solution.py:42
  210.7 0.0 copy-start
  210.7 9.0 %all_to_all.5 = f32[16,1,128]{2,1,0:T(1,128)S(1)} all-to-all(f32[16,1,128]{2,1,0:T(1,128)S(1)} %stack.3), channel_id=1, replica_groups=mesh['grp'=2,'seg'=16] {'seg'}, dimensions={0} | all-to-all | bytes 16384 | tf_op jit(solution)/shard_map/all_to_all | solution.py:68
  219.7 0.5 reduce_min.19
  220.3 0.0 copy-done
  (11 shorter events, 0.2 us)
Async XLA Ops:
  1.3 26.8 %collective-permute-start = (bf16[512]{0:T(512)(128)(2,1)S(1)}, bf16[512]{0:T(512)(128)(2,1)S(1)}, u32[]{:S(2)}, u32[]{:S(2)}) collective-permute-start(bf16[512]{0:T(512)(128)(2,1)S(1)} %slice.22), channel_id=1, source_target_pairs={{1,0},{2,1},{3,2},{4,3},{5,4},{6,5},{7,6},{8,7},{9,8},{10,9},{11,1... | collective-permute-start | bytes 3080 | tf_op jit(solution)/shard_map/ppermute | solution.py:12
  196.2 5.8 %slice-start = ((bf16[32,512,1025]{2,1,0:T(8,128)(2,1)}), bf16[32,512,512]{2,1,0:T(8,128)(2,1)S(1)}, s32[]{:S(2)}) async-start(bf16[32,512,1025]{2,1,0:T(8,128)(2,1)} %reshape.75), calls=%async_computation.1 | async-start | bytes 33554432 | tf_op jit(solution)/shard_map/slice | solution.py:21
  210.7 9.6 %copy-start = (f32[128]{0:T(128)}, f32[128]{0:T(128)S(1)}, u32[]{:S(2)}) copy-start(f32[128]{0:T(128)S(1)} %fusion.7) | copy-start | bytes 1540
